TPU v7x, 256 devices: a whole 4x4x8 slice. The times are simulated.
256 devices in a mesh: gx: 32 (over y, z), gy: 8 (over x, core).
Axes of the slice: x: 4, y: 4, z: 8, core: 2. Of those that a mesh axis runs over, the one named last changes fastest.
Arguments:
- density_init: float32 [2, 1024, 512, 128], P(None, 'gx', 'gy'), may hold values from 0.2 to 1.5
- solid_mask: int32 [1024, 512, 128], P('gx', 'gy'), may hold values from 0 to 1
- loadings: float32 [2], replicated, may hold values from 0.3 to 1
Outputs:
- density: float32 [2, 1024, 512, 128], P(None, 'gx', 'gy')
All inputs are finite; a program needn't handle non-finite values.
Results may differ from a plain program's by a relative error of at most 0.0001.
Values sent between devices are 32-bit elements; how exact they have to be, the bound alone decides.
A program may use at most 128 MiB of HBM per device.

v0:
```python
import functools

import jax
import jax.numpy as jnp
import ml_dtypes
import numpy as np
from jax import lax
from jax.experimental import pallas as pl
from jax.experimental.pallas import tpu as pltpu
from jax.sharding import PartitionSpec as P

ITERS = 2
SEGMENTS = (1.5131, 1.0)
RADII = (6.0, 8.0)
CROSS = 0.25
DAMPING = 0.3
ATTRACT = ((0.3, 0.22), (0.22, 0.16))

W = 8
ROWS, COLS, DEPTH = 32, 64, 128
PR, PC = ROWS + 2 * W, COLS + 2 * W
BLK = 8
GX, GY, NZ_, NY_ = 32, 8, 8, 4
MESH = pl.DeviceIdType.MESH
BF16 = jnp.bfloat16
F32 = jnp.float32


def raw_profile(kind, radius):
    k = np.arange(17) - 8.0
    if kind == 0:
        return np.maximum(radius * radius - k * k, 0.0)
    if kind == 1:
        return k * k * np.maximum(radius * radius - k * k, 0.0)
    v = np.exp(-np.abs(k) / 4.0)
    return v / v.sum()


RAW = {(k, c): raw_profile(k, RADII[c]) for k in range(3) for c in range(2)}


def x_taps(kind, comp, extra=1.0):
    v = RAW[kind, comp]
    return (v / v.sum() ** 3 * extra).tolist()


def split_np(table):
    hi = table.astype(np.float32).astype(ml_dtypes.bfloat16)
    lo = (table - hi.astype(np.float64)).astype(np.float32).astype(ml_dtypes.bfloat16)
    return hi, lo


def band_y(profiles):
    tables = []
    for taps in profiles:
        t = np.zeros((COLS, PC))
        for o in range(COLS):
            t[o, o : o + 17] = taps
        tables.append(t)
    hi, lo = split_np(np.concatenate(tables, 0))
    pad = np.zeros((hi.shape[0], 16), ml_dtypes.bfloat16)
    return np.concatenate([hi, hi, lo, pad], 1)


def band_z(taps):
    t = np.zeros((DEPTH, DEPTH))
    for o in range(DEPTH):
        for k in range(17):
            i = o + k - 8
            if 0 <= i < DEPTH:
                t[i, o] = taps[k]
    return t


def stack_z(table):
    hi, lo = split_np(table)
    return np.concatenate([hi, hi, lo], 0)


def constants():
    ya = [band_y([RAW[0, c], RAW[1, c], RAW[2, c]]) for c in range(2)]
    yb = [band_y([RAW[k, 0], RAW[k, 1]]) for k in (1, 0)]
    zp = stack_z(np.concatenate([band_z(RAW[0, 0]), band_z(RAW[0, 1])], 0))[: 4 * DEPTH]
    zs = stack_z(np.concatenate([band_z(RAW[1, 0]), band_z(RAW[1, 1])], 0))
    a = band_z(RAW[2, 0])
    za = stack_z(
        np.concatenate(
            [np.concatenate([ATTRACT[i][j] * a for i in range(2)], 1) for j in range(2)], 0
        )
    )
    zm = [
        stack_z(np.concatenate([band_z(RAW[0, i]), band_z(RAW[1, i])], 0)) for i in range(2)
    ]
    return [np.stack(ya), np.stack(yb), zp, zs, za, np.stack(zm)]


def split(v):
    hi = v.astype(BF16)
    return hi, (v - hi.astype(F32)).astype(BF16)


def kernel(
    dens_hbm, mask_hbm, load_ref, ya_ref, yb_ref, zp_ref, zs_ref, za_ref, zm_ref,
    out_ref,
    rho, prp, der1, der2, mask, yf, lh, res, att, tot, scl, arbuf, arrecv,
    in_sem, hs, hr, cs, cr, as_, ar_,
):
    gx, gy = lax.axis_index("gx"), lax.axis_index("gy")
    yy, zz = gx // NZ_, gx % NZ_
    cells = float(ROWS * GX * COLS * GY * DEPTH)

    loads = [
        pltpu.make_async_copy(
            dens_hbm, rho.at[:, pl.ds(W, ROWS), pl.ds(W, COLS), :], in_sem.at[0]
        ),
        pltpu.make_async_copy(mask_hbm, mask, in_sem.at[1]),
    ]
    for c in loads:
        c.start()

    group_peers = (
        [(gx, (gy + d) % GY) for d in range(1, GY)]
        + [(yy * NZ_ + (zz + d) % NZ_, gy) for d in range(1, NZ_)]
        + [(((yy + d) % NY_) * NZ_ + zz, gy) for d in range(1, NY_)]
    )
    barrier = pltpu.get_barrier_semaphore()
    for peer in group_peers:
        pl.semaphore_signal(barrier, inc=1, device_id=peer, device_id_type=MESH)

    has_lo, has_hi = gx > 0, gx < GX - 1
    has_l, has_r = gy > 0, gy < GY - 1

    @pl.when(has_lo)
    def _():
        pl.semaphore_signal(barrier, inc=1, device_id=(gx - 1, gy), device_id_type=MESH)

    @pl.when(has_hi)
    def _():
        pl.semaphore_signal(barrier, inc=1, device_id=(gx + 1, gy), device_id_type=MESH)

    for buf in (rho, prp, der1, der2):
        @pl.when(gx == 0)
        def _(buf=buf):
            buf[:, pl.ds(0, W)] = jnp.zeros((2, W, PC, DEPTH), F32)

        @pl.when(gx == GX - 1)
        def _(buf=buf):
            buf[:, pl.ds(W + ROWS, W)] = jnp.zeros((2, W, PC, DEPTH), F32)

        @pl.when(gy == 0)
        def _(buf=buf):
            buf[:, :, pl.ds(0, W)] = jnp.zeros((2, PR, W, DEPTH), F32)

        @pl.when(gy == GY - 1)
        def _(buf=buf):
            buf[:, :, pl.ds(W + COLS, W)] = jnp.zeros((2, PR, W, DEPTH), F32)

    for c in loads:
        c.wait()

    def mask_row(x, carry):
        keep = mask[x] == 0
        for c in range(2):
            v = rho[c, x + W, pl.ds(W, COLS), :]
            rho[c, x + W, pl.ds(W, COLS), :] = jnp.where(keep, v, 0.0)
        return carry

    lax.fori_loop(0, ROWS, mask_row, 0)

    pl.semaphore_wait(
        barrier, len(group_peers) + has_lo.astype(jnp.int32) + has_hi.astype(jnp.int32)
    )

    def copy(buf, src, dst, send, recv, peer):
        return pltpu.make_async_remote_copy(
            src_ref=buf.at[(slice(None),) + src],
            dst_ref=buf.at[(slice(None),) + dst],
            send_sem=send,
            recv_sem=recv,
            device_id=peer,
            device_id_type=MESH,
        )

    def exchange(n, buf, w):
        own_x, own_y = pl.ds(W, ROWS), pl.ds(W, COLS)
        lo_src, hi_src = pl.ds(W, w), pl.ds(W + ROWS - w, w)
        lo_dst, hi_dst = pl.ds(W - w, w), pl.ds(W + ROWS, w)
        l_src, r_src = pl.ds(W, W), pl.ds(COLS, W)
        l_dst, r_dst = pl.ds(0, W), pl.ds(W + COLS, W)
        down, up = (gx - 1, gy), (gx + 1, gy)
        left, right = (gx, gy - 1), (gx, gy + 1)
        faces = [
            (copy(buf, (lo_src, own_y), (hi_dst, own_y), hs.at[n, 0], hr.at[n, 0], down), has_lo, has_hi),
            (copy(buf, (hi_src, own_y), (lo_dst, own_y), hs.at[n, 1], hr.at[n, 1], up), has_hi, has_lo),
            (copy(buf, (own_x, l_src), (own_x, r_dst), hs.at[n, 2], hr.at[n, 2], left), has_l, has_r),
            (copy(buf, (own_x, r_src), (own_x, l_dst), hs.at[n, 3], hr.at[n, 3], right), has_r, has_l),
        ]
        corners = []
        for i, (rows, has_x) in enumerate(((lo_dst, has_lo), (hi_dst, has_hi))):
            corners.append(
                (copy(buf, (rows, l_src), (rows, r_dst), cs.at[n, 2 * i], cr.at[n, 2 * i], left),
                 has_x & has_l, has_x & has_r)
            )
            corners.append(
                (copy(buf, (rows, r_src), (rows, l_dst), cs.at[n, 2 * i + 1], cr.at[n, 2 * i + 1], right),
                 has_x & has_r, has_x & has_l)
            )
        return faces, corners

    def start(items):
        for c, to, _ in items:
            pl.when(to)(c.start)

    def wait_recv(items):
        for c, _, frm in items:
            pl.when(frm)(c.wait_recv)

    def wait_send(items):
        for c, to, _ in items:
            pl.when(to)(c.wait_send)

    def conv_y(buf, band_ref, order, lo, hi):
        def pair(p, carry):
            x = 2 * p
            for ch, fields in order:
                columns = []
                for j in range(2):
                    h, l = split(buf[ch, x + j])
                    columns.append(jnp.concatenate([h, l, h, h[:16]], 0))
                rhs = jnp.concatenate(columns, 1)
                out = jnp.dot(band_ref[ch], rhs, preferred_element_type=F32)
                for q, f in enumerate(fields):
                    for j in range(2):
                        yf[f, x + j] = out[q * COLS : (q + 1) * COLS, j * DEPTH : (j + 1) * DEPTH]
            return carry

        lax.fori_loop(lo, hi, pair, 0)

    def conv_x(b, specs):
        def chunk(j, carry):
            cols = pl.ds(pl.multiple_of(j * 16, 16), 16)
            for f, taps, radius, kind, column in specs:
                rows = {
                    i: yf[f, b * BLK + W + i, cols, :] for i in range(-radius, BLK + radius)
                }
                for x in range(BLK):
                    acc = None
                    for k in range(radius + 1):
                        w = taps[8 + k]
                        if w == 0.0:
                            continue
                        v = rows[x] if k == 0 else rows[x + k] + rows[x - k]
                        acc = w * v if acc is None else acc + w * v
                    h, l = split(acc)
                    at = pl.ds(pl.multiple_of(x * COLS + j * 16, 16), 16)
                    lh[kind, 0, at, pl.ds(column * DEPTH, DEPTH)] = h
                    lh[kind, 1, at, pl.ds(column * DEPTH, DEPTH)] = l
            return carry

        lax.fori_loop(0, COLS // 16, chunk, 0)

    def conv_z(kind, band_ref_value, terms):
        h, l = lh[kind, 0], lh[kind, 1]
        lhs = jnp.concatenate([h, l, h][:terms], 1)
        return jnp.dot(lhs, band_ref_value, preferred_element_type=F32)

    specs_a = []
    for c, r in ((0, 5), (1, 7)):
        specs_a.append((c * 3 + 0, x_taps(0, c, SEGMENTS[c]), r, 0, c))
        specs_a.append((c * 3 + 1, x_taps(1, c), r, 1, c))
        specs_a.append((c * 3 + 2, x_taps(2, c), 8, 2, c))
    specs_b = []
    for c, r in ((0, 5), (1, 7)):
        specs_b.append((2 + c, x_taps(0, c, SEGMENTS[c]), r, c, 0))
        specs_b.append((c, x_taps(1, c), r, c, 1))

    def stage_a(b, der):
        conv_x(b, specs_a)
        res[0] = conv_z(0, zp_ref[...], 2)
        res[1] = conv_z(1, zs_ref[...], 3)
        both = conv_z(2, za_ref[...], 3)
        at = pl.ds(pl.multiple_of(b * BLK * COLS, BLK * COLS), BLK * COLS)
        att[0, at] = both[:, :DEPTH]
        att[1, at] = both[:, DEPTH:]

        def row(x, carry):
            at = pl.ds(pl.multiple_of(x * COLS, COLS), COLS)
            t = 1.0 + res[0, at]
            n2 = res[1, at]
            der[0, b * BLK + x + W, pl.ds(W, COLS), :] = jnp.log(t) + (2.0 * CROSS) * n2 * t
            der[1, b * BLK + x + W, pl.ds(W, COLS), :] = n2 / t + CROSS * n2 * n2
            return carry

        lax.fori_loop(0, BLK, row, 0)

    def stage_b(b):
        conv_x(b, specs_b)
        for i in range(2):
            res[i] = conv_z(i, zm_ref[i], 3)

        def row(x, carry):
            at = pl.ds(pl.multiple_of(x * COLS, COLS), COLS)
            glob = pl.ds(pl.multiple_of((b * BLK + x) * COLS, COLS), COLS)
            keep = mask[b * BLK + x] == 0
            for i in range(2):
                v = jnp.where(keep, jnp.exp(att[i, glob] - res[i, at]), 0.0)
                prp[i, b * BLK + x + W, pl.ds(W, COLS), :] = v
                part = v[0:8]
                for q in range(1, COLS // 8):
                    part = part + v[8 * q : 8 * q + 8]
                tot[i] = tot[i] + part
            return carry

        lax.fori_loop(0, BLK, row, 0)

    def total_scales(it):
        sums = [jnp.sum(tot[i], axis=0, keepdims=True) for i in range(2)]
        rowid = lax.broadcasted_iota(jnp.int32, (8, DEPTH), 0)
        mine = jnp.where(rowid == 0, sums[0], jnp.where(rowid == 1, sums[1], 0.0))
        stages = [
            [(gx, (gy + d) % GY) for d in range(1, GY)],
            [(yy * NZ_ + (zz + d) % NZ_, gy) for d in range(1, NZ_)],
            [(((yy + d) % NY_) * NZ_ + zz, gy) for d in range(1, NY_)],
        ]
        copies = []
        for s, peers in enumerate(stages):
            arbuf[it, s] = mine
            sent = []
            for d, peer in enumerate(peers):
                c = pltpu.make_async_remote_copy(
                    src_ref=arbuf.at[it, s],
                    dst_ref=arrecv.at[it, s, d],
                    send_sem=as_.at[it, s, d],
                    recv_sem=ar_.at[it, s, d],
                    device_id=peer,
                    device_id_type=MESH,
                )
                c.start()
                sent.append(c)
            for d, c in enumerate(sent):
                c.wait_recv()
                mine = mine + arrecv[it, s, d]
            copies += sent
        total = jnp.sum(mine, axis=1, keepdims=True)
        for i in range(2):
            s = load_ref[i] * cells / total[i : i + 1]
            scl[i] = jnp.broadcast_to(s, (8, DEPTH))
        return copies

    order_a = ((0, (0, 1, 2)), (1, (3, 4, 5)))
    order_b = ((0, (0, 1)), (1, (2, 3)))
    pending = []
    ders = (der1, der2)
    source = rho
    first = exchange(0, rho, W)
    start(first[0])
    for it in range(ITERS):
        faces, corners = first
        pending += [faces, corners]
        wait_recv(faces)
        start(corners)
        if it == 1:
            wait_recv(corners)
            for c in copies:
                c.wait_send()
            wait_send(pending[0])
            wait_send(pending[1])

            def mix(x, carry):
                for c in range(2):
                    rho[c, x] = (1.0 - DAMPING) * rho[c, x] + (DAMPING * scl[c, 0:1]) * prp[c, x]
                return carry

            lax.fori_loop(0, PR, mix, 0)
        else:
            wait_recv(corners)
        conv_y(rho, ya_ref, order_a, 0, PR // 2)
        der = ders[it]
        lax.fori_loop(0, ROWS // BLK, lambda b, carry: (stage_a(b, der), carry)[1], 0)
        faces, corners = exchange(1 + 2 * it, der, W - 1)
        pending += [faces, corners]
        start(faces)
        wait_recv(faces)
        start(corners)
        wait_recv(corners)
        conv_y(der, yb_ref, order_b, 0, PR // 2)
        tot[...] = jnp.zeros_like(tot)
        if it == 1:
            wait_send(pending[4])
            wait_send(pending[5])
        lax.fori_loop(0, ROWS // BLK, lambda b, carry: (stage_b(b), carry)[1], 0)
        if it == 0:
            first = exchange(2, prp, W)
            start(first[0])
        copies = total_scales(it)
    for c in copies:
        c.wait_send()
    wait_send(pending[2])
    wait_send(pending[3])
    wait_send(pending[6])
    wait_send(pending[7])

    def final(x, carry):
        for c in range(2):
            out_ref[c, x] = (1.0 - DAMPING) * rho[c, x + W, pl.ds(W, COLS), :] + (
                DAMPING * scl[c, 0:1]
            ) * prp[c, x + W, pl.ds(W, COLS), :]
        return carry

    lax.fori_loop(0, ROWS, final, 0)


def body(density_init, solid_mask, loadings):
    consts = [jnp.asarray(c) for c in constants()]
    anyspace = pl.BlockSpec(memory_space=pl.ANY)
    vmem = pl.BlockSpec(memory_space=pltpu.VMEM)
    smem = pl.BlockSpec(memory_space=pltpu.SMEM)
    padded = pltpu.VMEM((2, PR, PC, DEPTH), F32)
    dma = pltpu.SemaphoreType.DMA
    return pl.pallas_call(
        kernel,
        out_shape=jax.ShapeDtypeStruct((2, ROWS, COLS, DEPTH), F32),
        in_specs=[anyspace, anyspace, smem] + [vmem] * len(consts),
        out_specs=vmem,
        scratch_shapes=[
            padded, padded, padded, padded,
            pltpu.VMEM((ROWS, COLS, DEPTH), jnp.int32),
            pltpu.VMEM((6, PR, COLS, DEPTH), F32),
            pltpu.VMEM((3, 2, BLK * COLS, 2 * DEPTH), BF16),
            pltpu.VMEM((2, BLK * COLS, DEPTH), F32),
            pltpu.VMEM((2, ROWS * COLS, DEPTH), F32),
            pltpu.VMEM((2, 8, DEPTH), F32),
            pltpu.VMEM((2, 8, DEPTH), F32),
            pltpu.VMEM((2, 3, 8, DEPTH), F32),
            pltpu.VMEM((2, 3, 7, 8, DEPTH), F32),
            dma((2,)),
            dma((4, 4)), dma((4, 4)), dma((4, 4)), dma((4, 4)),
            dma((2, 3, 7)), dma((2, 3, 7)),
        ],
        compiler_params=pltpu.CompilerParams(
            collective_id=0, has_side_effects=True, vmem_limit_bytes=60 * 2**20
        ),
        name="picard",
    )(density_init, solid_mask, loadings, *consts)


def solution(mesh):
    in_specs = (P(None, "gx", "gy", None), P("gx", "gy", None), P())
    out_specs = P(None, "gx", "gy", None)
    return jax.shard_map(body, mesh=mesh, in_specs=in_specs, out_specs=out_specs, check_vma=False)
```

profile of v0, /device:TPU:1, one launch (start us, length us, event | category | flops | bytes accessed | tf_op | source)
XLA Modules:
  0.0 145.1 jit_solution(2382798601218513640)
XLA Ops:
  0.0 141.9 %picard.1 = f32[2,32,64,128]{3,2,1,0:T(8,128)} custom-call(f32[2,32,64,128]{3,2,1,0:T(8,128)} %dens_hbm.1, s32[32,64,128]{2,1,0:T(8,128)} %mask_hbm.1, f32[2]{0:T(128)} %load_ref.1, bf16[2,192,256]{2,1,0:T(8,128)(2,1)} %constant.12.clone.ya_ref, bf16[2,128,256]{2,1,0:T(8,128)(2,1)} %constant.13.clone.yb_ref, bf16[512,128]{1,0:T(8,128)(2,1)} %constant.14.clone.zp_ref, ...), custom_call_target="tpu_custom_call" | custom-call | tf_op jit(solution)/shard_map/picard/pallas_call | solution.py:420
  141.9 3.2 %copy.11 = f32[2,32,64,128]{3,2,1,0:T(8,128)} copy(f32[2,32,64,128]{3,2,1,0:T(8,128)} %picard.1) | data formatting | bytes 4194304
where the time goes:
time: 145 us
  Pallas kernels  142 us (98%)
  local copies, waits for them, and re-layouts  3.16 us (2%)
    pallas_call x1, Pallas kernels, body(): pl.pallas_call(kernel, out_shape=jax.ShapeDtypeStruct((2, ROWS, COLS, DEP...  142 us
    unnamed x1, local copies, waits for them, and re-layouts  3.16 us

commit v1 on v0

v1 whole, which is shorter than its diff:
```python
import functools

import jax
import jax.numpy as jnp
import ml_dtypes
import numpy as np
from jax import lax
from jax.experimental import pallas as pl
from jax.experimental.pallas import tpu as pltpu
from jax.sharding import PartitionSpec as P

ITERS = 2
SEGMENTS = (1.5131, 1.0)
RADII = (6.0, 8.0)
CROSS = 0.25
DAMPING = 0.3
ATTRACT = ((0.3, 0.22), (0.22, 0.16))

W = 8
ROWS, COLS, DEPTH = 32, 64, 128
PR, PC = ROWS + 2 * W, COLS + 2 * W
BLK = 8
GX, GY, NZ_, NY_ = 32, 8, 8, 4
MESH = pl.DeviceIdType.MESH
BF16 = jnp.bfloat16
F32 = jnp.float32


def raw_profile(kind, radius):
    k = np.arange(17) - 8.0
    if kind == 0:
        return np.maximum(radius * radius - k * k, 0.0)
    if kind == 1:
        return k * k * np.maximum(radius * radius - k * k, 0.0)
    v = np.exp(-np.abs(k) / 4.0)
    return v / v.sum()


RAW = {(k, c): raw_profile(k, RADII[c]) for k in range(3) for c in range(2)}


def x_taps(kind, comp, extra=1.0):
    v = RAW[kind, comp]
    return (v / v.sum() ** 3 * extra).tolist()


def split_np(table):
    hi = table.astype(np.float32).astype(ml_dtypes.bfloat16)
    lo = (table - hi.astype(np.float64)).astype(np.float32).astype(ml_dtypes.bfloat16)
    return hi, lo


def band_y(profiles):
    tables = []
    for taps in profiles:
        t = np.zeros((COLS, PC))
        for o in range(COLS):
            t[o, o : o + 17] = taps
        tables.append(t)
    hi, lo = split_np(np.concatenate(tables, 0))
    pad = np.zeros((hi.shape[0], 16), ml_dtypes.bfloat16)
    return np.concatenate([hi, hi, lo, pad], 1)


def band_z(taps):
    t = np.zeros((DEPTH, DEPTH))
    for o in range(DEPTH):
        for k in range(17):
            i = o + k - 8
            if 0 <= i < DEPTH:
                t[i, o] = taps[k]
    return t


def stack_z(table):
    hi, lo = split_np(table)
    return np.concatenate([hi, hi, lo], 0)


def constants():
    ya = [band_y([RAW[0, c], RAW[1, c], RAW[2, c]]) for c in range(2)]
    yb = [band_y([RAW[k, 0], RAW[k, 1]]) for k in (1, 0)]
    zp = stack_z(np.concatenate([band_z(RAW[0, 0]), band_z(RAW[0, 1])], 0))[: 4 * DEPTH]
    zs = stack_z(np.concatenate([band_z(RAW[1, 0]), band_z(RAW[1, 1])], 0))
    a = band_z(RAW[2, 0])
    za = stack_z(
        np.concatenate(
            [np.concatenate([ATTRACT[i][j] * a for i in range(2)], 1) for j in range(2)], 0
        )
    )
    zm = [
        stack_z(np.concatenate([band_z(RAW[0, i]), band_z(RAW[1, i])], 0)) for i in range(2)
    ]
    return [np.stack(ya), np.stack(yb), zp, zs, za, np.stack(zm)]


def split(v):
    hi = v.astype(BF16)
    return hi, (v - hi.astype(F32)).astype(BF16)


def kernel(
    dens_hbm, mask_hbm, load_ref, ya_hbm, yb_hbm, zp_hbm, zs_hbm, za_hbm, zm_hbm,
    base_ref, prop_ref, scl_ref,
    rho, prp, der1, der2, mask, yfa, yfp, yfb, lh, res, att, tot, scl, arbuf, arrecv,
    ya_ref, yb_ref, zp_ref, zs_ref, za_ref, zm_ref,
    in_sem, hs, hr, as_, ar_,
):
    gx, gy = lax.axis_index("gx"), lax.axis_index("gy")
    yy, zz = gx // NZ_, gx % NZ_
    cells = float(ROWS * GX * COLS * GY * DEPTH)

    loads = [
        pltpu.make_async_copy(
            dens_hbm, rho.at[:, pl.ds(W, ROWS), pl.ds(W, COLS), :], in_sem.at[0]
        ),
        pltpu.make_async_copy(mask_hbm, mask, in_sem.at[1]),
    ]
    tables = [
        pltpu.make_async_copy(a, b, in_sem.at[2 + i])
        for i, (a, b) in enumerate(
            (
                (ya_hbm, ya_ref), (zp_hbm, zp_ref), (zs_hbm, zs_ref),
                (za_hbm, za_ref), (yb_hbm, yb_ref), (zm_hbm, zm_ref),
            )
        )
    ]
    for c in loads + tables:
        c.start()

    stages = [
        [(gx, (gy + d) % GY) for d in range(1, GY)],
        [(yy * NZ_ + (zz + d) % NZ_, gy) for d in range(1, NZ_)],
        [(((yy + d) % NY_) * NZ_ + zz, gy) for d in range(1, NY_)],
    ]
    barrier = pltpu.get_barrier_semaphore()
    greeted = 0
    for peers in stages:
        for peer in peers:
            greeted += 1
            pl.semaphore_signal(barrier, inc=1, device_id=peer, device_id_type=MESH)

    has_lo, has_hi = gx > 0, gx < GX - 1
    has_l, has_r = gy > 0, gy < GY - 1

    @pl.when(has_lo)
    def _():
        pl.semaphore_signal(barrier, inc=1, device_id=(gx - 1, gy), device_id_type=MESH)

    @pl.when(has_hi)
    def _():
        pl.semaphore_signal(barrier, inc=1, device_id=(gx + 1, gy), device_id_type=MESH)

    for buf in (rho, prp, der1, der2):
        @pl.when(gx == 0)
        def _(buf=buf):
            buf[:, pl.ds(0, W)] = jnp.zeros((2, W, PC, DEPTH), F32)

        @pl.when(gx == GX - 1)
        def _(buf=buf):
            buf[:, pl.ds(W + ROWS, W)] = jnp.zeros((2, W, PC, DEPTH), F32)

        @pl.when(gy == 0)
        def _(buf=buf):
            buf[:, :, pl.ds(0, W)] = jnp.zeros((2, PR, W, DEPTH), F32)

        @pl.when(gy == GY - 1)
        def _(buf=buf):
            buf[:, :, pl.ds(W + COLS, W)] = jnp.zeros((2, PR, W, DEPTH), F32)

    tot[...] = jnp.zeros_like(tot)
    for c in loads:
        c.wait()

    def mask_row(x, carry):
        keep = mask[x] == 0
        for c in range(2):
            v = rho[c, x + W, pl.ds(W, COLS), :]
            rho[c, x + W, pl.ds(W, COLS), :] = jnp.where(keep, v, 0.0)
        return carry

    lax.fori_loop(0, ROWS, mask_row, 0)

    pl.semaphore_wait(
        barrier, greeted + has_lo.astype(jnp.int32) + has_hi.astype(jnp.int32)
    )

    class Exchange:
        def __init__(self, n, buf, w):
            count = [0]

            def item(src, dst, peer, to, frm):
                k = count[0]
                count[0] += 1
                c = pltpu.make_async_remote_copy(
                    src_ref=buf.at[(slice(None),) + src],
                    dst_ref=buf.at[(slice(None),) + dst],
                    send_sem=hs.at[n, k],
                    recv_sem=hr.at[n, k],
                    device_id=peer,
                    device_id_type=MESH,
                )
                return c, to, frm

            down, up = (gx - 1, gy), (gx + 1, gy)
            left, right = (gx, gy - 1), (gx, gy + 1)
            l_src, r_src = pl.ds(W, W), pl.ds(COLS, W)
            l_dst, r_dst = pl.ds(0, W), pl.ds(W + COLS, W)
            lo_dst, hi_dst = pl.ds(W - w, w), pl.ds(W + ROWS, w)
            parts = (l_src, r_src, pl.ds(2 * W, COLS - 2 * W))
            self.x = [
                [item((pl.ds(W, w), p), (hi_dst, p), down, has_lo, has_hi) for p in parts],
                [item((pl.ds(W + ROWS - w, w), p), (lo_dst, p), up, has_hi, has_lo) for p in parts],
            ]
            self.y = []
            for rows in (pl.ds(W, BLK), pl.ds(W + BLK, 2 * BLK), pl.ds(W + 3 * BLK, BLK)):
                self.y.append(
                    [
                        item((rows, l_src), (rows, r_dst), left, has_l, has_r),
                        item((rows, r_src), (rows, l_dst), right, has_r, has_l),
                    ]
                )
            self.corner = []
            for rows, has_x in ((lo_dst, has_lo), (hi_dst, has_hi)):
                self.corner.append(
                    [
                        item((rows, l_src), (rows, r_dst), left, has_x & has_l, has_x & has_r),
                        item((rows, r_src), (rows, l_dst), right, has_x & has_r, has_x & has_l),
                    ]
                )
            self.all = self.x[0] + self.x[1] + sum(self.y, []) + sum(self.corner, [])

        def send_side(self, side):
            start(self.x[side][:2])
            start(self.y[0 if side == 0 else 2])
            start(self.x[side][2:])

        def forward(self, side):
            recv(self.x[1 - side][:2])
            start(self.corner[side])

        def finish(self, side):
            recv(self.x[1 - side][2:])
            recv(self.corner[side])

    def start(items):
        for c, to, _ in items:
            pl.when(to)(c.start)

    def recv(items):
        for c, _, frm in items:
            pl.when(frm)(c.wait_recv)

    def sent(items):
        for c, to, _ in items:
            pl.when(to)(c.wait_send)

    def conv_y(buf, band_ref, yf, order, lo, hi, mixed=False):
        def pair(p, carry):
            x = 2 * p
            for ch, fields in order:
                columns = []
                for j in range(2):
                    h, l = split(buf[ch, x + j])
                    columns.append(jnp.concatenate([h, l, h, h[:16]], 0))
                rhs = jnp.concatenate(columns, 1)
                out = jnp.dot(band_ref[ch], rhs, preferred_element_type=F32)
                for q, f in enumerate(fields):
                    for j in range(2):
                        v = out[q * COLS : (q + 1) * COLS, j * DEPTH : (j + 1) * DEPTH]
                        if mixed:
                            v = (1.0 - DAMPING) * yf[f, x + j] + scl[ch, 0:1] * v
                        yf[f, x + j] = v
            return carry

        lax.fori_loop(lo, hi, pair, 0)

    def conv_x(b, yf, specs):
        def chunk(j, carry):
            cols = pl.ds(pl.multiple_of(j * 16, 16), 16)
            for f, taps, radius, kind, column in specs:
                rows = {
                    i: yf[f, b * BLK + W + i, cols, :] for i in range(-radius, BLK + radius)
                }
                for x in range(BLK):
                    acc = None
                    for k in range(radius + 1):
                        w = taps[8 + k]
                        if w == 0.0:
                            continue
                        v = rows[x] if k == 0 else rows[x + k] + rows[x - k]
                        acc = w * v if acc is None else acc + w * v
                    h, l = split(acc)
                    at = pl.ds(pl.multiple_of(x * COLS + j * 16, 16), 16)
                    lh[kind, 0, at, pl.ds(column * DEPTH, DEPTH)] = h
                    lh[kind, 1, at, pl.ds(column * DEPTH, DEPTH)] = l
            return carry

        lax.fori_loop(0, COLS // 16, chunk, 0)

    def conv_z(kind, table, terms):
        h, l = lh[kind, 0], lh[kind, 1]
        lhs = jnp.concatenate([h, l, h][:terms], 1)
        return jnp.dot(lhs, table, preferred_element_type=F32)

    specs_a = []
    for c, r in ((0, 5), (1, 7)):
        specs_a.append((c * 3 + 0, x_taps(0, c, SEGMENTS[c]), r, 0, c))
        specs_a.append((c * 3 + 1, x_taps(1, c), r, 1, c))
        specs_a.append((c * 3 + 2, x_taps(2, c), 8, 2, c))
    specs_b = []
    for c, r in ((0, 5), (1, 7)):
        specs_b.append((2 + c, x_taps(0, c, SEGMENTS[c]), r, c, 0))
        specs_b.append((c, x_taps(1, c), r, c, 1))

    def stage_a(lo, hi, der):
        def one(b, carry):
            conv_x(b, yfa, specs_a)
            res[0] = conv_z(0, zp_ref[...], 2)
            res[1] = conv_z(1, zs_ref[...], 3)
            both = conv_z(2, za_ref[...], 3)
            at = pl.ds(pl.multiple_of(b * BLK * COLS, BLK * COLS), BLK * COLS)
            att[0, at] = both[:, :DEPTH]
            att[1, at] = both[:, DEPTH:]

            def row(x, carry):
                at = pl.ds(pl.multiple_of(x * COLS, COLS), COLS)
                t = 1.0 + res[0, at]
                n2 = res[1, at]
                der[0, b * BLK + x + W, pl.ds(W, COLS), :] = jnp.log(t) + (2.0 * CROSS) * n2 * t
                der[1, b * BLK + x + W, pl.ds(W, COLS), :] = n2 / t + CROSS * n2 * n2
                return carry

            lax.fori_loop(0, BLK, row, 0)
            return carry

        lax.fori_loop(lo, hi, one, 0)

    def stage_b(lo, hi, dest, off):
        def one(b, carry):
            conv_x(b, yfb, specs_b)
            for i in range(2):
                res[i] = conv_z(i, zm_ref[i], 3)

            def row(x, carry):
                at = pl.ds(pl.multiple_of(x * COLS, COLS), COLS)
                glob = pl.ds(pl.multiple_of((b * BLK + x) * COLS, COLS), COLS)
                keep = mask[b * BLK + x] == 0
                for i in range(2):
                    v = jnp.where(keep, jnp.exp(att[i, glob] - res[i, at]), 0.0)
                    dest[i, b * BLK + x + off, pl.ds(off, COLS), :] = v
                    part = v[0:8]
                    for q in range(1, COLS // 8):
                        part = part + v[8 * q : 8 * q + 8]
                    tot[i] = tot[i] + part
                return carry

            lax.fori_loop(0, BLK, row, 0)
            return carry

        lax.fori_loop(lo, hi, one, 0)

    copies = []

    def sum_start(it, s, mine):
        arbuf[it, s] = mine
        out = []
        for d, peer in enumerate(stages[s]):
            c = pltpu.make_async_remote_copy(
                src_ref=arbuf.at[it, s],
                dst_ref=arrecv.at[it, s, d],
                send_sem=as_.at[it, s, d],
                recv_sem=ar_.at[it, s, d],
                device_id=peer,
                device_id_type=MESH,
            )
            c.start()
            out.append(c)
        copies.extend(out)
        return out

    def sum_finish(it, s, mine, out):
        for d, c in enumerate(out):
            c.wait_recv()
            mine = mine + arrecv[it, s, d]
        return mine

    def local_total():
        sums = [jnp.sum(tot[i], axis=0, keepdims=True) for i in range(2)]
        rowid = lax.broadcasted_iota(jnp.int32, (8, DEPTH), 0)
        return jnp.where(rowid == 0, sums[0], jnp.where(rowid == 1, sums[1], 0.0))

    def scales(mine, dest):
        total = jnp.sum(mine, axis=1, keepdims=True)
        for i in range(2):
            dest[i] = jnp.broadcast_to(DAMPING * load_ref[i] * cells / total[i : i + 1], (8, DEPTH))

    order_a = ((0, (0, 1, 2)), (1, (3, 4, 5)))
    order_b = ((0, (0, 1)), (1, (2, 3)))
    x_rho = Exchange(0, rho, W)
    x_der1 = Exchange(1, der1, W - 1)
    x_prp = Exchange(2, prp, W)
    x_der2 = Exchange(3, der2, W - 1)
    HALF = (0, 4), (20, 24)

    for side in range(2):
        start(x_rho.x[side][:2])
    for side in range(2):
        start(x_rho.x[side][2:])
    for part in range(3):
        start(x_rho.y[part])
    tables[0].wait()
    for part in range(3):
        recv(x_rho.y[part])
    conv_y(rho, ya_ref, yfa, order_a, 4, 12)
    x_rho.forward(0)
    x_rho.forward(1)
    conv_y(rho, ya_ref, yfa, order_a, 12, 20)
    for t in tables[1:4]:
        t.wait()
    stage_a(1, 3, der1)
    start(x_der1.y[1])
    for side in range(2):
        x_rho.finish(side)
        conv_y(rho, ya_ref, yfa, order_a, *HALF[side])
        stage_a(3 * side, 3 * side + 1, der1)
        x_der1.send_side(side)

    for t in tables[4:]:
        t.wait()
    recv(x_der1.y[1])
    conv_y(der1, yb_ref, yfb, order_b, 8, 16)
    recv(x_der1.y[0])
    conv_y(der1, yb_ref, yfb, order_b, 4, 8)
    x_der1.forward(1)
    recv(x_der1.y[2])
    conv_y(der1, yb_ref, yfb, order_b, 16, 20)
    x_der1.forward(0)
    stage_b(1, 3, prp, W)
    start(x_prp.y[1])
    for side in (1, 0):
        x_der1.finish(side)
        conv_y(der1, yb_ref, yfb, order_b, *HALF[side])
        stage_b(3 * side, 3 * side + 1, prp, W)
        x_prp.send_side(side)

    mine = local_total()
    tot[...] = jnp.zeros_like(tot)
    out = sum_start(0, 0, mine)
    recv(x_prp.y[1])
    conv_y(prp, ya_ref, yfp, order_a, 8, 16)
    mine = sum_finish(0, 0, mine, out)
    out = sum_start(0, 1, mine)
    recv(x_prp.y[2])
    recv(x_prp.y[0])
    x_prp.forward(0)
    conv_y(prp, ya_ref, yfp, order_a, 16, 20)
    mine = sum_finish(0, 1, mine, out)
    out = sum_start(0, 2, mine)
    x_prp.forward(1)
    conv_y(prp, ya_ref, yfp, order_a, 4, 8)
    mine = sum_finish(0, 2, mine, out)
    scales(mine, scl)

    def mix(x, carry):
        for f in range(6):
            yfa[f, x] = (1.0 - DAMPING) * yfa[f, x] + scl[f // 3, 0:1] * yfp[f, x]
        return carry

    lax.fori_loop(W, W + ROWS, mix, 0)
    for side in range(2):
        x_prp.finish(side)
        conv_y(prp, ya_ref, yfa, order_a, *HALF[side], mixed=True)
        stage_a(3 * side, 3 * side + 1, der2)
        x_der2.send_side(side)
    stage_a(1, 3, der2)
    start(x_der2.y[1])

    recv(x_der2.y[0])
    conv_y(der2, yb_ref, yfb, order_b, 4, 8)
    recv(x_der2.y[2])
    conv_y(der2, yb_ref, yfb, order_b, 16, 20)
    x_der2.forward(1)
    x_der2.forward(0)

    def base(x, carry):
        for c in range(2):
            new = (1.0 - DAMPING) * rho[c, x + W, pl.ds(W, COLS), :] + scl[c, 0:1] * prp[
                c, x + W, pl.ds(W, COLS), :
            ]
            base_ref[c, x] = (1.0 - DAMPING) * new
        return carry

    lax.fori_loop(0, ROWS, base, 0)
    recv(x_der2.y[1])
    conv_y(der2, yb_ref, yfb, order_b, 8, 16)
    stage_b(1, 3, prop_ref, 0)
    for side in (1, 0):
        x_der2.finish(side)
        conv_y(der2, yb_ref, yfb, order_b, *HALF[side])
        stage_b(3 * side, 3 * side + 1, prop_ref, 0)
    mine = local_total()
    for s in range(3):
        out = sum_start(1, s, mine)
        mine = sum_finish(1, s, mine, out)
    scales(mine, scl_ref)

    for x in (x_rho, x_der1, x_prp, x_der2):
        sent(x.all)
    for c in copies:
        c.wait_send()


def last_kernel(base_ref, prop_ref, scl_ref, out_hbm, buf, sem):
    step = 8
    copies = []
    for x in range(0, ROWS, step):

        def row(i, carry):
            for c in range(2):
                buf[c, i] = base_ref[c, i] + scl_ref[c, 0:1] * prop_ref[c, i]
            return carry

        lax.fori_loop(x, x + step, row, 0)
        at = pl.ds(x, step)
        c = pltpu.make_async_copy(buf.at[:, at], out_hbm.at[:, at], sem.at[x // step])
        c.start()
        copies.append(c)
    for c in copies:
        c.wait()


def body(density_init, solid_mask, loadings):
    consts = [jnp.asarray(c) for c in constants()]
    anyspace = pl.BlockSpec(memory_space=pl.ANY)
    vmem = pl.BlockSpec(memory_space=pltpu.VMEM)
    smem = pl.BlockSpec(memory_space=pltpu.SMEM)
    padded = pltpu.VMEM((2, PR, PC, DEPTH), F32)
    field = pltpu.VMEM((2, ROWS, COLS, DEPTH), F32)
    dma = pltpu.SemaphoreType.DMA
    base, prop, scl = pl.pallas_call(
        kernel,
        out_shape=(field, field, pltpu.VMEM((2, 8, DEPTH), F32)),
        in_specs=[anyspace, anyspace, smem] + [anyspace] * len(consts),
        out_specs=(vmem, vmem, vmem),
        scratch_shapes=[
            padded, padded, padded, padded,
            pltpu.VMEM((ROWS, COLS, DEPTH), jnp.int32),
            pltpu.VMEM((6, PR, COLS, DEPTH), F32),
            pltpu.VMEM((6, PR, COLS, DEPTH), F32),
            pltpu.VMEM((4, PR, COLS, DEPTH), F32),
            pltpu.VMEM((3, 2, BLK * COLS, 2 * DEPTH), BF16),
            pltpu.VMEM((2, BLK * COLS, DEPTH), F32),
            pltpu.VMEM((2, ROWS * COLS, DEPTH), F32),
            pltpu.VMEM((2, 8, DEPTH), F32),
            pltpu.VMEM((2, 8, DEPTH), F32),
            pltpu.VMEM((2, 3, 8, DEPTH), F32),
            pltpu.VMEM((2, 3, 7, 8, DEPTH), F32),
        ]
        + [pltpu.VMEM(c.shape, BF16) for c in consts]
        + [dma((8,)), dma((4, 16)), dma((4, 16)), dma((2, 3, 7)), dma((2, 3, 7))],
        compiler_params=pltpu.CompilerParams(
            collective_id=0, has_side_effects=True, vmem_limit_bytes=54 * 2**20
        ),
        name="picard",
    )(density_init, solid_mask, loadings, *consts)
    return pl.pallas_call(
        last_kernel,
        out_shape=jax.ShapeDtypeStruct((2, ROWS, COLS, DEPTH), F32),
        in_specs=[vmem, vmem, vmem],
        out_specs=anyspace,
        scratch_shapes=[field, dma((4,))],
        compiler_params=pltpu.CompilerParams(vmem_limit_bytes=4 * 2**20),
        name="last",
    )(base, prop, scl)


def solution(mesh):
    in_specs = (P(None, "gx", "gy", None), P("gx", "gy", None), P())
    out_specs = P(None, "gx", "gy", None)
    return jax.shard_map(body, mesh=mesh, in_specs=in_specs, out_specs=out_specs, check_vma=False)
```

time: 145 us -> 101 us (0.70)
  Pallas kernels: 142 us -> 101 us
  local copies, waits for them, and re-layouts: 3.16 us -> 0 us
    pallas_call x1 -> x2, Pallas kernels: 142 us -> 101 us  [the longest x1 99.1 us: body(): pl.pallas_call(kernel, out_shape=(field, field, pltpu.VMEM((2, 8, DEPTH),...]
    unnamed x1 -> x0, local copies, waits for them, and re-layouts: 3.16 us -> none
where the time goes in v1:
time: 101 us
  Pallas kernels  101 us (100%)
    pallas_call x1, Pallas kernels, body(): pl.pallas_call(kernel, out_shape=(field, field, pltpu.VMEM((2, 8, DEPTH),...  99.1 us

profile of v1, /device:TPU:1, one launch (start us, length us, event | category | flops | bytes accessed | tf_op | source)
XLA Modules:
  0.0 100.5 jit_solution(16672918075606099653)
XLA Ops:
  0.0 99.1 %picard.1 = (f32[2,32,64,128]{3,2,1,0:T(8,128)S(1)}, f32[2,32,64,128]{3,2,1,0:T(8,128)S(1)}, f32[2,8,128]{2,1,0:T(8,128)S(1)}) custom-call(f32[2,32,64,128]{3,2,1,0:T(8,128)} %dens_hbm.1, s32[32,64,128]{2,1,0:T(8,128)} %mask_hbm.1, f32[2]{0:T(128)} %load_ref.1, bf16[2,192,256]{2,1,0:T(8,128)(2,1)} %constant.12.clone.ya_hbm, ...), custom_call_target="tpu_custom_call" | custom-call | tf_op jit(solution)/shard_map/picard/pallas_call | solution.py:541
  99.1 1.4 %last.1 = f32[2,32,64,128]{3,2,1,0:T(8,128)} custom-call(f32[2,32,64,128]{3,2,1,0:T(8,128)S(1)} %get-tuple-element.8.base_ref, f32[2,32,64,128]{3,2,1,0:T(8,128)S(1)} %get-tuple-element.9.prop_ref, f32[2,8,128]{2,1,0:T(8,128)S(1)} %get-tuple-element.10.scl_ref), custom_call_target="tpu_custom_call" | custom-call | tf_op jit(solution)/shard_map/last/pallas_call | solution.py:567

commit v2 on v1

v2 whole, which is shorter than its diff:
```python
import jax
import jax.numpy as jnp
import ml_dtypes
import numpy as np
from jax import lax
from jax.experimental import pallas as pl
from jax.experimental.pallas import tpu as pltpu
from jax.sharding import PartitionSpec as P

SEGMENTS = (1.5131, 1.0)
RADII = (6.0, 8.0)
CROSS = 0.25
DAMPING = 0.3
ATTRACT = ((0.3, 0.22), (0.22, 0.16))

W = 8
ROWS, COLS, DEPTH = 32, 64, 128
PR, PC = ROWS + 2 * W, COLS + 2 * W
BLK = 8
GX, GY, NZ_, NY_ = 32, 8, 8, 4
NEAR, FAR = 0, 1
HALF = 4
DECAY = float(np.exp(-0.25))
MESH = pl.DeviceIdType.MESH
BF16 = jnp.bfloat16
F32 = jnp.float32


def raw_profile(kind, radius):
    k = np.arange(17) - 8.0
    if kind == 0:
        return np.maximum(radius * radius - k * k, 0.0)
    if kind == 1:
        return k * k * np.maximum(radius * radius - k * k, 0.0)
    v = np.exp(-np.abs(k) / 4.0)
    return v / v.sum()


RAW = {(k, c): raw_profile(k, RADII[c]) for k in range(3) for c in range(2)}


def x_taps(kind, comp, extra=1.0):
    v = RAW[kind, comp]
    return (v / v.sum() ** 3 * extra).tolist()


def split_np(table):
    hi = table.astype(np.float32).astype(ml_dtypes.bfloat16)
    lo = (table - hi.astype(np.float64)).astype(np.float32).astype(ml_dtypes.bfloat16)
    return hi, lo


def band_y(profiles):
    tables = []
    for taps in profiles:
        t = np.zeros((COLS, PC))
        for o in range(COLS):
            t[o, o : o + 17] = taps
        tables.append(t)
    hi, lo = split_np(np.concatenate(tables, 0))
    pad = np.zeros((hi.shape[0], 16), ml_dtypes.bfloat16)
    return np.concatenate([hi, hi, lo, pad], 1)


def band_z(taps):
    t = np.zeros((DEPTH, DEPTH))
    for o in range(DEPTH):
        for k in range(17):
            i = o + k - 8
            if 0 <= i < DEPTH:
                t[i, o] = taps[k]
    return t


def wide_z(table):
    hi, lo = split_np(table)
    return np.concatenate(
        [np.concatenate([hi, lo], 1), np.concatenate([hi, np.zeros_like(lo)], 1)], 0
    )


def constants():
    ya = [band_y([RAW[0, c], RAW[1, c], RAW[2, c]]) for c in range(2)]
    yb = [band_y([RAW[k, 0], RAW[k, 1]]) for k in (1, 0)]
    zp = [np.concatenate([split_np(band_z(RAW[0, c]))[0]] * 2, 0) for c in range(2)]
    zs = [wide_z(band_z(RAW[1, c])) for c in range(2)]
    za = wide_z(band_z(RAW[2, 0]) * RAW[2, 0][8])
    return [np.stack(ya), np.stack(yb), np.stack(zp), np.stack(zs), za]


def split(v):
    hi = v.astype(BF16)
    return hi, (v - hi.astype(F32)).astype(BF16)


def kernel(
    dens_hbm, mask_hbm, load_ref, ya_hbm, yb_hbm, zp_hbm, zs_hbm, za_hbm,
    base_ref, prop_ref, scl_ref,
    rho, prp, der1, der2, mask, yfa, yfb, lh, res, cres, att, tot, scl, arbuf, arrecv,
    ya_ref, yb_ref, zp_ref, zs_ref, za_ref,
    in_sem, hs, hr, as_, ar_,
):
    gx, gy = lax.axis_index("gx"), lax.axis_index("gy")
    yy, zz = gx // NZ_, gx % NZ_
    cells = float(ROWS * GX * COLS * GY * DEPTH)

    loads = [
        pltpu.make_async_copy(
            dens_hbm, rho.at[:, pl.ds(W, ROWS), pl.ds(W, COLS), :], in_sem.at[0]
        ),
        pltpu.make_async_copy(mask_hbm, mask, in_sem.at[1]),
    ]
    wanted = (
        (ya_hbm, ya_ref), (zp_hbm, zp_ref), (zs_hbm, zs_ref), (za_hbm, za_ref), (yb_hbm, yb_ref),
    )
    tables = [
        pltpu.make_async_copy(a, b, in_sem.at[2 + i]) for i, (a, b) in enumerate(wanted)
    ]
    for c in loads + tables:
        c.start()

    xx, core = gy // 2, gy % 2
    stages = [
        [(yy * NZ_ + (zz + d // 2) % NZ_, xx * 2 + (core + d) % 2) for d in range(1, 16)],
        [(((yy + d // 4) % NY_) * NZ_ + zz, ((xx + d) % 4) * 2 + core) for d in range(1, 16)],
    ]
    barrier = pltpu.get_barrier_semaphore()
    greeted = 0
    for peers in stages:
        for peer in peers:
            greeted += 1
            pl.semaphore_signal(barrier, inc=1, device_id=peer, device_id_type=MESH)

    has_lo, has_hi = gx > 0, gx < GX - 1
    has_l, has_r = gy > 0, gy < GY - 1

    near = (
        (has_lo, (gx - 1, gy)),
        (has_hi, (gx + 1, gy)),
        (has_l, (gx, gy - 1)),
        (has_r, (gx, gy + 1)),
    )
    for there, peer in near:
        @pl.when(there)
        def _(peer=peer):
            pl.semaphore_signal(barrier, inc=1, device_id=peer, device_id_type=MESH)

    def zeros(buf):
        @pl.when(gx == 0)
        def _():
            buf[:, pl.ds(0, W)] = jnp.zeros((2, W, PC, DEPTH), F32)

        @pl.when(gx == GX - 1)
        def _():
            buf[:, pl.ds(W + ROWS, W)] = jnp.zeros((2, W, PC, DEPTH), F32)

        @pl.when(gy == 0)
        def _():
            buf[:, :, pl.ds(0, W)] = jnp.zeros((2, PR, W, DEPTH), F32)

        @pl.when(gy == GY - 1)
        def _():
            buf[:, :, pl.ds(W + COLS, W)] = jnp.zeros((2, PR, W, DEPTH), F32)

    zeros(rho)
    for c in loads:
        c.wait()

    def mask_row(x, carry):
        keep = mask[x] == 0
        for c in range(2):
            v = rho[c, x + W, pl.ds(W, COLS), :]
            rho[c, x + W, pl.ds(W, COLS), :] = jnp.where(keep, v, 0.0)
        return carry

    lax.fori_loop(0, ROWS, mask_row, 0)

    pl.semaphore_wait(
        barrier, greeted + sum(there.astype(jnp.int32) for there, _ in near)
    )

    with_both = [(x & has_l, x & has_r) for x in (has_lo, has_hi)]

    class Exchange:
        def __init__(self, n, buf, w):
            count = [0]

            def item(src, dst, peer, to, frm):
                k = count[0]
                count[0] += 1
                c = pltpu.make_async_remote_copy(
                    src_ref=buf.at[(slice(None),) + src],
                    dst_ref=buf.at[(slice(None),) + dst],
                    send_sem=hs.at[n, k],
                    recv_sem=hr.at[n, k],
                    device_id=peer,
                    device_id_type=MESH,
                )
                return c, to, frm

            down, up = (gx - 1, gy), (gx + 1, gy)
            left, right = (gx, gy - 1), (gx, gy + 1)
            l_src, r_src = pl.ds(W, W), pl.ds(COLS, W)
            l_dst, r_dst = pl.ds(0, W), pl.ds(W + COLS, W)
            parts = (l_src, r_src, pl.ds(2 * W, COLS - 2 * W))
            lo_rows = ((0, HALF), (HALF, w - HALF))
            hi_rows = ((ROWS - HALF, HALF), (ROWS - w, w - HALF))
            self.x = [[], []]
            self.corner = [[], []]
            for r, k in lo_rows:
                src, dst = pl.ds(W + r, k), pl.ds(W + ROWS + r, k)
                self.x[0].append([item((src, p), (dst, p), down, has_lo, has_hi) for p in parts])
            for r, k in hi_rows:
                src, dst = pl.ds(W + r, k), pl.ds(W + r - ROWS, k)
                self.x[1].append([item((src, p), (dst, p), up, has_hi, has_lo) for p in parts])
            for side, rows, shift in ((0, hi_rows, -ROWS), (1, lo_rows, ROWS)):
                with_l, with_r = with_both[side]
                for r, k in rows:
                    at = pl.ds(W + r + shift, k)
                    self.corner[side].append(
                        [
                            item((at, l_src), (at, r_dst), left, with_l, with_r),
                            item((at, r_src), (at, l_dst), right, with_r, with_l),
                        ]
                    )
            self.y = []
            for r, k in ((0, 4), (4, 4), (8, 16), (24, 4), (28, 4)):
                at = pl.ds(W + r, k)
                self.y.append(
                    [
                        item((at, l_src), (at, r_dst), left, has_l, has_r),
                        item((at, r_src), (at, l_dst), right, has_r, has_l),
                    ]
                )
            self.all = sum(self.x[0] + self.x[1] + self.corner[0] + self.corner[1] + self.y, [])

        def send(self, side, c):
            start(self.x[side][c] + self.y[((0, 1), (4, 3))[side][c]])

        def forward(self, side, c):
            recv(self.x[1 - side][c][:2])
            start(self.corner[side][c])

        def finish(self, side, c):
            recv(self.x[1 - side][c][2:] + self.corner[side][c])

    def grouped(items, which, act):
        groups = {}
        for item in items:
            groups.setdefault(id(item[which]), []).append(item)
        for group in groups.values():
            @pl.when(group[0][which])
            def _(group=group):
                for item in group:
                    act(item[0])

    def start(items):
        grouped(items, 1, lambda c: c.start())

    def recv(items):
        grouped(items, 2, lambda c: c.wait_recv())

    def sent(items):
        grouped(items, 1, lambda c: c.wait_send())

    def conv_y(buf, band_ref, yf, order, lo, hi):
        def pair(p, carry):
            x = 2 * p
            for ch, fields in order:
                columns = []
                for j in range(2):
                    h, l = split(buf[ch, x + j])
                    columns.append(jnp.concatenate([h, l, h, h[:16]], 0))
                rhs = jnp.concatenate(columns, 1)
                out = jnp.dot(band_ref[ch], rhs, preferred_element_type=F32)
                for q, f in enumerate(fields):
                    for j in range(2):
                        yf[f, x + j] = out[q * COLS : (q + 1) * COLS, j * DEPTH : (j + 1) * DEPTH]
            return carry

        lax.fori_loop(lo, hi, pair, 0, unroll=2)

    def decaying(rows, n):
        q, q9 = DECAY, DECAY**9
        ahead, behind = [None] * n, [None] * n
        acc = rows[-8]
        for k in range(-7, 1):
            acc = acc * q + rows[k]
        behind[0] = acc
        for x in range(1, n):
            acc = acc * q + (rows[x] - q9 * rows[x - 9])
            behind[x] = acc
        acc = rows[n + 7]
        for k in range(n + 6, n - 1, -1):
            acc = acc * q + rows[k]
        acc = acc * q
        ahead[n - 1] = acc
        for x in range(n - 2, -1, -1):
            acc = (acc + rows[x + 1]) * q - q9 * rows[x + 9]
            ahead[x] = acc
        return [a + b for a, b in zip(ahead, behind)]

    def conv_x(r0, n, yf, specs):
        def chunk(j, carry):
            cols = pl.ds(pl.multiple_of(j * 16, 16), 16)
            for f, taps, radius, kind, comp in specs:
                rows = {i: yf[f, r0 + W + i, cols, :] for i in range(-radius, n + radius)}
                if taps is None:
                    outs = decaying(rows, n)
                else:
                    outs = []
                    for x in range(n):
                        acc = None
                        for k in range(radius + 1):
                            w = taps[8 + k]
                            if w == 0.0:
                                continue
                            v = rows[x] if k == 0 else rows[x + k] + rows[x - k]
                            acc = w * v if acc is None else acc + w * v
                        outs.append(acc)
                for x in range(n):
                    h, l = split(outs[x])
                    at = pl.ds(pl.multiple_of(x * COLS + j * 16, 16), 16)
                    lh[kind, comp, at, pl.ds(0, DEPTH)] = h
                    lh[kind, comp, at, pl.ds(DEPTH, DEPTH)] = l
            return carry

        lax.fori_loop(0, COLS // 16, chunk, 0)

    def conv_z(kind, comp, n, table):
        v = jnp.dot(lh[kind, comp, pl.ds(0, n * COLS)], table, preferred_element_type=F32)
        return v if v.shape[1] == DEPTH else v[:, :DEPTH] + v[:, DEPTH:]

    specs_a = []
    for c, r in ((0, 5), (1, 7)):
        specs_a.append((c * 3 + 0, x_taps(0, c, SEGMENTS[c]), r, 0, c))
        specs_a.append((c * 3 + 1, x_taps(1, c), r, 1, c))
        specs_a.append((c * 3 + 2, None, 8, 2, c))
    specs_b = []
    for c, r in ((0, 5), (1, 7)):
        specs_b.append((2 + c, x_taps(0, c, SEGMENTS[c]), r, 0, c))
        specs_b.append((c, x_taps(1, c), r, 1, c))

    def convs_a(it, r0, n):
        conv_x(r0, n, yfa, specs_a)
        at = pl.ds(r0 * COLS, n * COLS)
        for c in range(2):
            lanes = pl.ds(c * DEPTH, DEPTH)
            cres[it, 0, at, lanes] = conv_z(0, c, n, zp_ref[c])
            cres[it, 1, at, lanes] = conv_z(1, c, n, zs_ref[c])
            cres[it, 2, at, lanes] = conv_z(2, c, n, za_ref[...])

    def derive(it, r0, n, der):
        def row(x, carry):
            at = pl.ds(pl.multiple_of(x * COLS, COLS), COLS)

            def both(kind):
                out = []
                for c in range(2):
                    lanes = pl.ds(c * DEPTH, DEPTH)
                    v = cres[0, kind, at, lanes]
                    if it == 1:
                        v = (1.0 - DAMPING) * v + scl[c, 0:1] * cres[1, kind, at, lanes]
                    out.append(v)
                return out

            p0, p1 = both(0)
            s0, s1 = both(1)
            a0, a1 = both(2)
            t = 1.0 + (p0 + p1)
            n2 = s0 + s1
            der[0, x + W, pl.ds(W, COLS), :] = jnp.log(t) + (2.0 * CROSS) * n2 * t
            der[1, x + W, pl.ds(W, COLS), :] = n2 / t + CROSS * n2 * n2
            for i in range(2):
                att[i, at] = ATTRACT[i][0] * a0 + ATTRACT[i][1] * a1
            return carry

        lax.fori_loop(r0, r0 + n, row, 0)

    def stage_a(it, r0, n, der):
        convs_a(it, r0, n)
        derive(it, r0, n, der)

    def stage_b(r0, n, dest, off):
        conv_x(r0, n, yfb, specs_b)
        for i in range(2):
            res[i, pl.ds(0, n * COLS)] = conv_z(0, i, n, zp_ref[i]) + conv_z(1, i, n, zs_ref[i])

        def row(x, carry):
            at = pl.ds(pl.multiple_of(x * COLS, COLS), COLS)
            glob = pl.ds(pl.multiple_of((r0 + x) * COLS, COLS), COLS)
            keep = mask[r0 + x] == 0
            for i in range(2):
                v = jnp.where(keep, jnp.exp(att[i, glob] - res[i, at]), 0.0)
                dest[i, r0 + x + off, pl.ds(off, COLS), :] = v
                part = v[0:8]
                for q in range(1, COLS // 8):
                    part = part + v[8 * q : 8 * q + 8]
                tot[i] = tot[i] + part
            return carry

        lax.fori_loop(0, n, row, 0)

    copies = []

    def sum_start(it, s, mine):
        arbuf[it, s] = mine
        out = []
        for d, peer in enumerate(stages[s]):
            c = pltpu.make_async_remote_copy(
                src_ref=arbuf.at[it, s],
                dst_ref=arrecv.at[it, s, d],
                send_sem=as_.at[it, s, d],
                recv_sem=ar_.at[it, s, d],
                device_id=peer,
                device_id_type=MESH,
            )
            c.start()
            out.append(c)
        copies.extend(out)
        return out

    def sum_finish(it, s, mine, out):
        for d, c in enumerate(out):
            c.wait_recv()
            mine = mine + arrecv[it, s, d]
        return mine

    def local_total():
        sums = [jnp.sum(tot[i], axis=0, keepdims=True) for i in range(2)]
        rowid = lax.broadcasted_iota(jnp.int32, (8, DEPTH), 0)
        return jnp.where(rowid == 0, sums[0], jnp.where(rowid == 1, sums[1], 0.0))

    def scales(mine, dest):
        total = jnp.sum(mine, axis=1, keepdims=True)
        for i in range(2):
            dest[i] = jnp.broadcast_to(DAMPING * load_ref[i] * cells / total[i : i + 1], (8, DEPTH))

    order_a = ((0, (0, 1, 2)), (1, (3, 4, 5)))
    order_b = ((0, (0, 1)), (1, (2, 3)))
    x_rho = Exchange(0, rho, W)
    x_der1 = Exchange(1, der1, W - 1)
    x_prp = Exchange(2, prp, W)
    x_der2 = Exchange(3, der2, W - 1)
    pairs = (((2, 4), (0, 2)), ((20, 22), (22, 24)))
    first = ((0, HALF), (ROWS - HALF, ROWS - 2 * HALF))
    sides = (0, 1)

    for c in (NEAR, FAR):
        for side in sides:
            x_rho.send(side, c)
    start(x_rho.y[2])
    for buf in (der1, prp, der2):
        zeros(buf)
    tot[...] = jnp.zeros_like(tot)
    tables[0].wait()
    recv(sum(x_rho.y, []))
    conv_y(rho, ya_ref, yfa, order_a, 4, 12)
    for side in sides:
        x_rho.forward(side, NEAR)
    conv_y(rho, ya_ref, yfa, order_a, 12, 20)
    for t in tables[1:4]:
        t.wait()
    stage_a(0, 8, 8, der1)
    for side in sides:
        x_rho.forward(side, FAR)
    stage_a(0, 16, 8, der1)
    start(x_der1.y[2])
    for side in sides:
        x_rho.finish(side, NEAR)
        conv_y(rho, ya_ref, yfa, order_a, *pairs[side][NEAR])
        stage_a(0, first[side][FAR], HALF, der1)
        x_der1.send(side, FAR)
    for side in sides:
        x_rho.finish(side, FAR)
        conv_y(rho, ya_ref, yfa, order_a, *pairs[side][FAR])
        stage_a(0, first[side][NEAR], HALF, der1)
        x_der1.send(side, NEAR)

    def proposals(x_der, der, dest, off, between, after):
        recv(x_der.y[2])
        conv_y(der, yb_ref, yfb, order_b, 8, 16)
        for side in sides:
            x_der.forward(side, FAR)
        recv(x_der.y[1])
        conv_y(der, yb_ref, yfb, order_b, 6, 8)
        recv(x_der.y[3])
        conv_y(der, yb_ref, yfb, order_b, 16, 18)
        recv(x_der.y[0])
        conv_y(der, yb_ref, yfb, order_b, 4, 6)
        recv(x_der.y[4])
        conv_y(der, yb_ref, yfb, order_b, 18, 20)
        stage_b(8, 8, dest, off)
        for side in sides:
            x_der.forward(side, NEAR)
        stage_b(16, 8, dest, off)
        between()
        for side in sides:
            x_der.finish(side, FAR)
            conv_y(der, yb_ref, yfb, order_b, *pairs[side][FAR])
        for side in sides:
            x_der.finish(side, NEAR)
            conv_y(der, yb_ref, yfb, order_b, *pairs[side][NEAR])
            stage_b(first[side][NEAR], HALF, dest, off)
            after(side, NEAR)
        for side in sides:
            stage_b(first[side][FAR], HALF, dest, off)
            after(side, FAR)

    for t in tables[4:]:
        t.wait()
    proposals(x_der1, der1, prp, W, lambda: start(x_prp.y[2]), x_prp.send)

    mine = local_total()
    tot[...] = jnp.zeros_like(tot)
    out = sum_start(0, 0, mine)
    recv(x_prp.y[2])
    conv_y(prp, ya_ref, yfa, order_a, 8, 16)
    recv(x_prp.y[0] + x_prp.y[4] + x_prp.y[1] + x_prp.y[3])
    conv_y(prp, ya_ref, yfa, order_a, 4, 8)
    for side in sides:
        x_prp.forward(side, NEAR)
    conv_y(prp, ya_ref, yfa, order_a, 16, 20)
    mine = sum_finish(0, 0, mine, out)
    out = sum_start(0, 1, mine)
    convs_a(1, 8, 8)
    for side in sides:
        x_prp.forward(side, FAR)
    convs_a(1, 16, 8)
    for side in sides:
        x_prp.finish(side, NEAR)
        conv_y(prp, ya_ref, yfa, order_a, *pairs[side][NEAR])
        convs_a(1, first[side][FAR], HALF)
    mine = sum_finish(0, 1, mine, out)
    scales(mine, scl)
    for side in sides:
        derive(1, first[side][FAR], HALF, der2)
        x_der2.send(side, FAR)
    derive(1, 8, 16, der2)
    start(x_der2.y[2])
    for side in sides:
        x_prp.finish(side, FAR)
        conv_y(prp, ya_ref, yfa, order_a, *pairs[side][FAR])
        convs_a(1, first[side][NEAR], HALF)
        derive(1, first[side][NEAR], HALF, der2)
        x_der2.send(side, NEAR)

    def base():
        def row(x, carry):
            for c in range(2):
                new = (1.0 - DAMPING) * rho[c, x + W, pl.ds(W, COLS), :] + scl[c, 0:1] * prp[
                    c, x + W, pl.ds(W, COLS), :
                ]
                base_ref[c, x] = (1.0 - DAMPING) * new
            return carry

        lax.fori_loop(0, ROWS, row, 0)

    proposals(x_der2, der2, prop_ref, 0, base, lambda side, c: None)
    mine = local_total()
    out = sum_start(1, 0, mine)
    sent(x_rho.all + x_der1.all + x_prp.all + x_der2.all)
    mine = sum_finish(1, 0, mine, out)
    out = sum_start(1, 1, mine)
    for c in copies[: -len(out)]:
        c.wait_send()
    mine = sum_finish(1, 1, mine, out)
    scales(mine, scl_ref)
    for c in out:
        c.wait_send()


def last_kernel(base_ref, prop_ref, scl_ref, out_hbm, buf, sem):
    step = 8
    copies = []
    for x in range(0, ROWS, step):

        def row(i, carry):
            for c in range(2):
                buf[c, i] = base_ref[c, i] + scl_ref[c, 0:1] * prop_ref[c, i]
            return carry

        lax.fori_loop(x, x + step, row, 0)
        at = pl.ds(x, step)
        c = pltpu.make_async_copy(buf.at[:, at], out_hbm.at[:, at], sem.at[x // step])
        c.start()
        copies.append(c)
    for c in copies:
        c.wait()


def body(density_init, solid_mask, loadings):
    consts = [jnp.asarray(c) for c in constants()]
    anyspace = pl.BlockSpec(memory_space=pl.ANY)
    vmem = pl.BlockSpec(memory_space=pltpu.VMEM)
    smem = pl.BlockSpec(memory_space=pltpu.SMEM)
    padded = pltpu.VMEM((2, PR, PC, DEPTH), F32)
    field = pltpu.VMEM((2, ROWS, COLS, DEPTH), F32)
    dma = pltpu.SemaphoreType.DMA
    base, prop, scl = pl.pallas_call(
        kernel,
        out_shape=(field, field, pltpu.VMEM((2, 8, DEPTH), F32)),
        in_specs=[anyspace, anyspace, smem] + [anyspace] * len(consts),
        out_specs=(vmem, vmem, vmem),
        scratch_shapes=[
            padded, padded, padded, padded,
            pltpu.VMEM((ROWS, COLS, DEPTH), jnp.int32),
            pltpu.VMEM((6, PR, COLS, DEPTH), F32),
            pltpu.VMEM((4, PR, COLS, DEPTH), F32),
            pltpu.VMEM((3, 2, BLK * COLS, 2 * DEPTH), BF16),
            pltpu.VMEM((2, BLK * COLS, DEPTH), F32),
            pltpu.VMEM((2, 3, ROWS * COLS, 2 * DEPTH), F32),
            pltpu.VMEM((2, ROWS * COLS, DEPTH), F32),
            pltpu.VMEM((2, 8, DEPTH), F32),
            pltpu.VMEM((2, 8, DEPTH), F32),
            pltpu.VMEM((2, 2, 8, DEPTH), F32),
            pltpu.VMEM((2, 2, 15, 8, DEPTH), F32),
        ]
        + [pltpu.VMEM(c.shape, BF16) for c in consts]
        + [dma((8,)), dma((4, 32)), dma((4, 32)), dma((2, 2, 15)), dma((2, 2, 15))],
        compiler_params=pltpu.CompilerParams(
            collective_id=0, has_side_effects=True, vmem_limit_bytes=54 * 2**20
        ),
        name="picard",
    )(density_init, solid_mask, loadings, *consts)
    return pl.pallas_call(
        last_kernel,
        out_shape=jax.ShapeDtypeStruct((2, ROWS, COLS, DEPTH), F32),
        in_specs=[vmem, vmem, vmem],
        out_specs=anyspace,
        scratch_shapes=[field, dma((4,))],
        compiler_params=pltpu.CompilerParams(vmem_limit_bytes=4 * 2**20),
        name="last",
    )(base, prop, scl)


def solution(mesh):
    in_specs = (P(None, "gx", "gy", None), P("gx", "gy", None), P())
    out_specs = P(None, "gx", "gy", None)
    return jax.shard_map(body, mesh=mesh, in_specs=in_specs, out_specs=out_specs, check_vma=False)
```

time: 101 us -> 93.4 us (0.925)
  Pallas kernels: 101 us -> 93.1 us
    pallas_call x1, Pallas kernels: 99.1 us -> 91.7 us  [body(): pl.pallas_call(kernel, out_shape=(field, field, pltpu.VMEM((2, 8, DEPTH),...]
where the time goes in v2:
time: 93.4 us; the launch traced here: 93.3 us
  Pallas kernels  93.1 us (100%)
    pallas_call x1, Pallas kernels, body(): pl.pallas_call(kernel, out_shape=(field, field, pltpu.VMEM((2, 8, DEPTH),...  91.7 us

profile of v2, /device:TPU:1, one launch (start us, length us, event | category | flops | bytes accessed | tf_op | source)
XLA Modules:
  0.0 93.3 jit_solution(6498666050170073479)
XLA Ops:
  0.0 91.7 %picard.1 = (f32[2,32,64,128]{3,2,1,0:T(8,128)S(1)}, f32[2,32,64,128]{3,2,1,0:T(8,128)S(1)}, f32[2,8,128]{2,1,0:T(8,128)S(1)}) custom-call(f32[2,32,64,128]{3,2,1,0:T(8,128)} %dens_hbm.1, s32[32,64,128]{2,1,0:T(8,128)} %mask_hbm.1, f32[2]{0:T(128)} %load_ref.1, bf16[2,192,256]{2,1,0:T(8,128)(2,1)} %constant.10.clone.ya_hbm, ...), custom_call_target="tpu_custom_call" | custom-call | tf_op jit(solution)/shard_map/picard/pallas_call | solution.py:600
  91.7 1.4 %last.1 = f32[2,32,64,128]{3,2,1,0:T(8,128)} custom-call(f32[2,32,64,128]{3,2,1,0:T(8,128)S(1)} %get-tuple-element.8.base_ref, f32[2,32,64,128]{3,2,1,0:T(8,128)S(1)} %get-tuple-element.9.prop_ref, f32[2,8,128]{2,1,0:T(8,128)S(1)} %get-tuple-element.10.scl_ref), custom_call_target="tpu_custom_call" | custom-call | tf_op jit(solution)/shard_map/last/pallas_call | solution.py:626

commit v3 on v2

--- a/solution.py
+++ b/solution.py
@@ -120,9 +120,13 @@
         c.start()
 
     xx, core = gy // 2, gy % 2
+    plane = [(dy, dx) for dy in range(NY_) for dx in range(4) if (dy, dx) != (0, 0)]
+    plane.sort(key=lambda p: -(min(p[0], NY_ - p[0]) + min(p[1], 4 - p[1])))
+    line = [(dz, dc) for dz in range(NZ_) for dc in range(2) if (dz, dc) != (0, 0)]
+    line.sort(key=lambda p: -(2 * min(p[0], NZ_ - p[0]) + p[1]))
     stages = [
-        [(yy * NZ_ + (zz + d // 2) % NZ_, xx * 2 + (core + d) % 2) for d in range(1, 16)],
-        [(((yy + d // 4) % NY_) * NZ_ + zz, ((xx + d) % 4) * 2 + core) for d in range(1, 16)],
+        [(((yy + dy) % NY_) * NZ_ + zz, ((xx + dx) % 4) * 2 + core) for dy, dx in plane],
+        [(yy * NZ_ + (zz + dz) % NZ_, xx * 2 + (core + dc) % 2) for dz, dc in line],
     ]
     barrier = pltpu.get_barrier_semaphore()
     greeted = 0
@@ -421,8 +425,8 @@
         return out
 
     def sum_finish(it, s, mine, out):
-        for d, c in enumerate(out):
-            c.wait_recv()
+        for d in range(len(out) - 1, -1, -1):
+            out[d].wait_recv()
             mine = mine + arrecv[it, s, d]
         return mine
 

time: 93.4 us -> 88 us (0.942)
  Pallas kernels: 93.1 us -> 87.7 us
    pallas_call x1, Pallas kernels: 91.7 us -> 86.3 us  [body(): pl.pallas_call(kernel, out_shape=(field, field, pltpu.VMEM((2, 8, DEPTH),...]
where the time goes in v3:
time: 88 us; the launch traced here: 87.9 us
  Pallas kernels  87.7 us (100%)
    pallas_call x1, Pallas kernels, body(): pl.pallas_call(kernel, out_shape=(field, field, pltpu.VMEM((2, 8, DEPTH),...  86.3 us

profile of v3, /device:TPU:1, one launch (start us, length us, event | category | flops | bytes accessed | tf_op | source)
XLA Modules:
  0.0 87.9 jit_solution(1049473440302533198)
XLA Ops:
  0.0 86.3 %picard.1 = (f32[2,32,64,128]{3,2,1,0:T(8,128)S(1)}, f32[2,32,64,128]{3,2,1,0:T(8,128)S(1)}, f32[2,8,128]{2,1,0:T(8,128)S(1)}) custom-call(f32[2,32,64,128]{3,2,1,0:T(8,128)} %dens_hbm.1, s32[32,64,128]{2,1,0:T(8,128)} %mask_hbm.1, f32[2]{0:T(128)} %load_ref.1, bf16[2,192,256]{2,1,0:T(8,128)(2,1)} %constant.10.clone.ya_hbm, ...), custom_call_target="tpu_custom_call" | custom-call | tf_op jit(solution)/shard_map/picard/pallas_call | solution.py:604
  86.3 1.4 %last.1 = f32[2,32,64,128]{3,2,1,0:T(8,128)} custom-call(f32[2,32,64,128]{3,2,1,0:T(8,128)S(1)} %get-tuple-element.8.base_ref, f32[2,32,64,128]{3,2,1,0:T(8,128)S(1)} %get-tuple-element.9.prop_ref, f32[2,8,128]{2,1,0:T(8,128)S(1)} %get-tuple-element.10.scl_ref), custom_call_target="tpu_custom_call" | custom-call | tf_op jit(solution)/shard_map/last/pallas_call | solution.py:630

commit v4 on v3

--- a/solution.py
+++ b/solution.py
@@ -329,7 +329,7 @@
                     lh[kind, comp, at, pl.ds(DEPTH, DEPTH)] = l
             return carry
 
-        lax.fori_loop(0, COLS // 16, chunk, 0)
+        lax.fori_loop(0, COLS // 16, chunk, 0, unroll=4 if n == HALF else 1)
 
     def conv_z(kind, comp, n, table):
         v = jnp.dot(lh[kind, comp, pl.ds(0, n * COLS)], table, preferred_element_type=F32)
@@ -347,7 +347,7 @@
 
     def convs_a(it, r0, n):
         conv_x(r0, n, yfa, specs_a)
-        at = pl.ds(r0 * COLS, n * COLS)
+        at = pl.ds(pl.multiple_of(r0 * COLS, HALF * COLS), n * COLS)
         for c in range(2):
             lanes = pl.ds(c * DEPTH, DEPTH)
             cres[it, 0, at, lanes] = conv_z(0, c, n, zp_ref[c])
@@ -355,7 +355,8 @@
             cres[it, 2, at, lanes] = conv_z(2, c, n, za_ref[...])
 
     def derive(it, r0, n, der):
-        def row(x, carry):
+        def row(i, carry):
+            x = r0 + i
             at = pl.ds(pl.multiple_of(x * COLS, COLS), COLS)
 
             def both(kind):
@@ -379,7 +380,7 @@
                 att[i, at] = ATTRACT[i][0] * a0 + ATTRACT[i][1] * a1
             return carry
 
-        lax.fori_loop(r0, r0 + n, row, 0)
+        lax.fori_loop(0, n, row, 0, unroll=2)
 
     def stage_a(it, r0, n, der):
         convs_a(it, r0, n)
@@ -403,7 +404,7 @@
                 tot[i] = tot[i] + part
             return carry
 
-        lax.fori_loop(0, n, row, 0)
+        lax.fori_loop(0, n, row, 0, unroll=2)
 
     copies = []
 
@@ -450,6 +451,18 @@
     first = ((0, HALF), (ROWS - HALF, ROWS - 2 * HALF))
     sides = (0, 1)
 
+    def inner(stage, between):
+        def step(i, carry):
+            stage(8 + 8 * i)
+            pl.when(i == 0)(between)
+            return carry
+
+        lax.fori_loop(0, 2, step, 0)
+
+    def forward(x, c):
+        for side in sides:
+            x.forward(side, c)
+
     for c in (NEAR, FAR):
         for side in sides:
             x_rho.send(side, c)
@@ -465,10 +478,7 @@
     conv_y(rho, ya_ref, yfa, order_a, 12, 20)
     for t in tables[1:4]:
         t.wait()
-    stage_a(0, 8, 8, der1)
-    for side in sides:
-        x_rho.forward(side, FAR)
-    stage_a(0, 16, 8, der1)
+    inner(lambda r0: stage_a(0, r0, 8, der1), lambda: forward(x_rho, FAR))
     start(x_der1.y[2])
     for side in sides:
         x_rho.finish(side, NEAR)
@@ -494,10 +504,7 @@
         conv_y(der, yb_ref, yfb, order_b, 4, 6)
         recv(x_der.y[4])
         conv_y(der, yb_ref, yfb, order_b, 18, 20)
-        stage_b(8, 8, dest, off)
-        for side in sides:
-            x_der.forward(side, NEAR)
-        stage_b(16, 8, dest, off)
+        inner(lambda r0: stage_b(r0, 8, dest, off), lambda: forward(x_der, NEAR))
         between()
         for side in sides:
             x_der.finish(side, FAR)
@@ -527,10 +534,7 @@
     conv_y(prp, ya_ref, yfa, order_a, 16, 20)
     mine = sum_finish(0, 0, mine, out)
     out = sum_start(0, 1, mine)
-    convs_a(1, 8, 8)
-    for side in sides:
-        x_prp.forward(side, FAR)
-    convs_a(1, 16, 8)
+    inner(lambda r0: convs_a(1, r0, 8), lambda: forward(x_prp, FAR))
     for side in sides:
         x_prp.finish(side, NEAR)
         conv_y(prp, ya_ref, yfa, order_a, *pairs[side][NEAR])

time: 88 us -> 85.4 us (0.970)
  Pallas kernels: 87.7 us -> 85.2 us
    pallas_call x1, Pallas kernels: 86.3 us -> 83.7 us  [body(): pl.pallas_call(kernel, out_shape=(field, field, pltpu.VMEM((2, 8, DEPTH),...]
where the time goes in v4:
time: 85.4 us; the launch traced here: 85.3 us
  Pallas kernels  85.2 us (100%)
    pallas_call x1, Pallas kernels, body(): pl.pallas_call(kernel, out_shape=(field, field, pltpu.VMEM((2, 8, DEPTH),...  83.7 us

profile of v4, /device:TPU:1, one launch (start us, length us, event | category | flops | bytes accessed | tf_op | source)
XLA Modules:
  0.0 85.3 jit_solution(7302348430689073625)
XLA Ops:
  0.0 83.7 %picard.1 = (f32[2,32,64,128]{3,2,1,0:T(8,128)S(1)}, f32[2,32,64,128]{3,2,1,0:T(8,128)S(1)}, f32[2,8,128]{2,1,0:T(8,128)S(1)}) custom-call(f32[2,32,64,128]{3,2,1,0:T(8,128)} %dens_hbm.1, s32[32,64,128]{2,1,0:T(8,128)} %mask_hbm.1, f32[2]{0:T(128)} %load_ref.1, bf16[2,192,256]{2,1,0:T(8,128)(2,1)} %constant.10.clone.ya_hbm, ...), custom_call_target="tpu_custom_call" | custom-call | tf_op jit(solution)/shard_map/picard/pallas_call | solution.py:608
  83.7 1.4 %last.1 = f32[2,32,64,128]{3,2,1,0:T(8,128)} custom-call(f32[2,32,64,128]{3,2,1,0:T(8,128)S(1)} %get-tuple-element.8.base_ref, f32[2,32,64,128]{3,2,1,0:T(8,128)S(1)} %get-tuple-element.9.prop_ref, f32[2,8,128]{2,1,0:T(8,128)S(1)} %get-tuple-element.10.scl_ref), custom_call_target="tpu_custom_call" | custom-call | tf_op jit(solution)/shard_map/last/pallas_call | solution.py:634

commit v5 on v4

--- a/solution.py
+++ b/solution.py
@@ -116,7 +116,7 @@
     tables = [
         pltpu.make_async_copy(a, b, in_sem.at[2 + i]) for i, (a, b) in enumerate(wanted)
     ]
-    for c in loads + tables:
+    for c in loads:
         c.start()
 
     xx, core = gy // 2, gy % 2
@@ -166,6 +166,8 @@
         def _():
             buf[:, :, pl.ds(W + COLS, W)] = jnp.zeros((2, PR, W, DEPTH), F32)
 
+    for c in tables:
+        c.start()
     zeros(rho)
     for c in loads:
         c.wait()
@@ -177,7 +179,7 @@
             rho[c, x + W, pl.ds(W, COLS), :] = jnp.where(keep, v, 0.0)
         return carry
 
-    lax.fori_loop(0, ROWS, mask_row, 0)
+    lax.fori_loop(0, ROWS, mask_row, 0, unroll=2)
 
     pl.semaphore_wait(
         barrier, greeted + sum(there.astype(jnp.int32) for there, _ in near)
@@ -329,7 +331,7 @@
                     lh[kind, comp, at, pl.ds(DEPTH, DEPTH)] = l
             return carry
 
-        lax.fori_loop(0, COLS // 16, chunk, 0, unroll=4 if n == HALF else 1)
+        lax.fori_loop(0, COLS // 16, chunk, 0, unroll=4 if n == HALF else 2)
 
     def conv_z(kind, comp, n, table):
         v = jnp.dot(lh[kind, comp, pl.ds(0, n * COLS)], table, preferred_element_type=F32)
@@ -539,9 +541,9 @@
         x_prp.finish(side, NEAR)
         conv_y(prp, ya_ref, yfa, order_a, *pairs[side][NEAR])
         convs_a(1, first[side][FAR], HALF)
-    mine = sum_finish(0, 1, mine, out)
-    scales(mine, scl)
-    for side in sides:
+        if side == 0:
+            mine = sum_finish(0, 1, mine, out)
+            scales(mine, scl)
         derive(1, first[side][FAR], HALF, der2)
         x_der2.send(side, FAR)
     derive(1, 8, 16, der2)

time: 85.4 us -> 86.1 us (level)
  no operation moved by 1% of the time
where the time goes in v5:
time: 86.1 us; the launch traced here: 86 us
  Pallas kernels  85.8 us (100%)
    pallas_call x1, Pallas kernels, body(): pl.pallas_call(kernel, out_shape=(field, field, pltpu.VMEM((2, 8, DEPTH),...  84.4 us

profile of v5, /device:TPU:1, one launch (start us, length us, event | category | flops | bytes accessed | tf_op | source)
XLA Modules:
  0.0 86.0 jit_solution(5421523160151467946)
XLA Ops:
  0.0 84.4 %picard.1 = (f32[2,32,64,128]{3,2,1,0:T(8,128)S(1)}, f32[2,32,64,128]{3,2,1,0:T(8,128)S(1)}, f32[2,8,128]{2,1,0:T(8,128)S(1)}) custom-call(f32[2,32,64,128]{3,2,1,0:T(8,128)} %dens_hbm.1, s32[32,64,128]{2,1,0:T(8,128)} %mask_hbm.1, f32[2]{0:T(128)} %load_ref.1, bf16[2,192,256]{2,1,0:T(8,128)(2,1)} %constant.10.clone.ya_hbm, ...), custom_call_target="tpu_custom_call" | custom-call | tf_op jit(solution)/shard_map/picard/pallas_call | solution.py:610
  84.4 1.4 %last.1 = f32[2,32,64,128]{3,2,1,0:T(8,128)} custom-call(f32[2,32,64,128]{3,2,1,0:T(8,128)S(1)} %get-tuple-element.8.base_ref, f32[2,32,64,128]{3,2,1,0:T(8,128)S(1)} %get-tuple-element.9.prop_ref, f32[2,8,128]{2,1,0:T(8,128)S(1)} %get-tuple-element.10.scl_ref), custom_call_target="tpu_custom_call" | custom-call | tf_op jit(solution)/shard_map/last/pallas_call | solution.py:636
